TPU v7x, 32 devices: a whole 2x2x4 slice. The times are simulated.
32 devices in a mesh: groups: 2 (over y), ctx: 4 (over z), exp: 4 (over x, core), rep: 1.
Axes of the slice: x: 2, y: 2, z: 4, core: 2. Of those that a mesh axis runs over, the one named last changes fastest.
Arguments:
- queries: bfloat16 [2, 256, 4096], P('groups', 'ctx', ('exp', 'rep')), parts along dimension 0, may hold values from -16.25 to 16.25
- pages: bfloat16 [2, 2304, 2, 512], P('groups', 'ctx', None, 'exp'), parts along dimension 0, may hold values from -5.2 to 5.2
- cached_lengths: int32 [2, 4], P('groups'), parts along dimension 0, may hold values from 128 to 512
- residual_in: bfloat16 [2, 256, 2048], P('groups', ('ctx', 'exp')), parts along dimension 0, may hold values from -2.390625 to 2.390625
- out_weight: bfloat16 [4096, 2048], P(('exp', 'rep')), may hold values from -0.09375 to 0.09375
- norm_gain: float32 [2048], replicated, may hold values from 0.1 to 1.9
- expert_ids: int32 [2, 256, 8], P('groups', ('ctx', 'exp')), parts along dimension 0, may hold values from 0 to 15, all different within a row; in each aligned block of 16 rows (0 to 15, 16 to 31, ..., all dimensions but the last counted through in order) at most 8 rows name the same one
- route_scores: float32 [2, 256, 8], P('groups', ('ctx', 'exp')), parts along dimension 0, may hold values from 0.05 to 1
- expert_input: bfloat16 [16, 2048, 2, 384], P(('ctx', 'exp'), None, None, 'rep'), may hold values from -0.125 to 0.125
- expert_output: bfloat16 [16, 384, 2048], P(('ctx', 'exp'), 'rep'), may hold values from -0.3125 to 0.3125
Outputs:
- context: bfloat16 [2, 256, 4096], P('groups', 'ctx', ('exp', 'rep')), parts along dimension 0
- layer_out: bfloat16 [2, 256, 2048], P('groups', ('ctx', 'exp', 'rep')), parts along dimension 0
There are 2 independent parts, one for each index of `groups`. A program takes and returns all parts, laid end to end along the dimension named above; an argument that names none is the same for every part. Nothing has to cross between parts.
Inputs may be any that keep to these rules, and one draw needn't show every extreme that they name: `expert_ids`: in every aligned block of 16 positions of one request, no expert is named by more than 8 of the block's rows, and in some blocks one expert by exactly 8; the 8 experts of a row differ.
All inputs are finite; a program needn't handle non-finite values.
Results may differ from a plain program's by a relative error of at most 0.015.
Values may be sent and summed in bfloat16 or wider, within the bound.
A program may use at most 128 MiB of HBM per device.

v0:
```python
import jax
import jax.numpy as jnp
from jax import lax
from jax.sharding import PartitionSpec as P

HEAD = 128
floor_value = -1e30
norm_epsilon = 1e-06


def normalize(hidden, norm_gain):
    widened = hidden.astype(jnp.float32)
    mean_square = jnp.mean(widened * widened, axis=-1, keepdims=True)
    return (widened * lax.rsqrt(mean_square + norm_epsilon) * norm_gain).astype(jnp.bfloat16)


def attend_piece(query_rows, page_rows, allowed):
    scaling = query_rows.shape[-1] ** (-0.5)
    scores = (
        jnp.einsum(
            "rqhe,rke->rqhk", query_rows, page_rows[:, :, 0], preferred_element_type=jnp.float32
        )
        * scaling
    )
    permitted = allowed[:, :, None, :]
    masked = jnp.where(permitted, scores, floor_value)
    peaks = jnp.max(masked, axis=-1)
    weights = jnp.where(permitted, jnp.exp(masked - peaks[..., None]), 0.0)
    totals = jnp.sum(weights, axis=-1)
    summed = jnp.einsum(
        "rqhk,rke->rqhe",
        weights.astype(jnp.bfloat16),
        page_rows[:, :, 1],
        preferred_element_type=jnp.float32,
    )
    return (peaks, totals, summed)


def merge_partials(earlier, later):
    peaks = jnp.maximum(earlier[0], later[0])
    later_scale = jnp.exp(later[0] - peaks)
    totals = later[1] * later_scale
    summed = later[2] * later_scale[..., None]
    return (peaks, totals, summed)


def rows_mask(row_index, lengths, query_positions, slab_size, fresh_block):
    page_size = slab_size + fresh_block
    page_number = row_index // page_size
    offset = row_index - page_number * page_size
    page_count = lengths.shape[1]
    picker = page_number[None, :] == jnp.arange(page_count, dtype=jnp.int32)[:, None]
    live_length = jnp.sum(jnp.where(picker[None], lengths[:, :, None], 0), axis=1)
    in_cache = (offset < slab_size)[None, :] & (offset[None, :] < live_length)
    fresh_position = page_number * fresh_block + offset - slab_size
    in_fresh = (offset >= slab_size)[None, :] & (
        fresh_position[None, :] <= query_positions[:, None]
    )
    return in_cache[:, None, :] | in_fresh[None, :, :]


def per_device(
    queries,
    pages,
    cached_lengths,
    residual_in,
    out_weight,
    norm_gain,
    expert_ids,
    route_scores,
    expert_input,
    expert_output,
):
    requests, fresh_block, query_width = queries.shape
    local_heads = query_width // HEAD
    core_place = lax.axis_index("rep")
    page_place = lax.axis_index("ctx")
    rep_count = lax.axis_size("rep")
    page_size = pages.shape[1]
    slab_size = page_size - fresh_block
    own_positions = page_place * fresh_block + jnp.arange(fresh_block, dtype=jnp.int32)
    query_rows = queries.reshape(requests, fresh_block, local_heads, HEAD)
    start_state = (
        jnp.full((requests, fresh_block, local_heads), floor_value, jnp.float32),
        jnp.zeros((requests, fresh_block, local_heads), jnp.float32),
        jnp.zeros((requests, fresh_block, local_heads, HEAD), jnp.float32),
    )
    page_piece = lax.all_gather(pages, "ctx", axis=1, tiled=True)
    row_index = jnp.arange(page_piece.shape[1], dtype=jnp.int32)
    allowed = rows_mask(row_index, cached_lengths, own_positions, slab_size, fresh_block)
    peaks, totals, summed = merge_partials(
        start_state, attend_piece(query_rows, page_piece, allowed)
    )
    context = (
        (summed / totals[..., None])
        .astype(jnp.bfloat16)
        .reshape(requests, fresh_block, query_width)
    )
    projected = jnp.dot(
        context.reshape(requests * fresh_block, query_width),
        out_weight,
        preferred_element_type=jnp.float32,
    ).reshape(requests, fresh_block, -1)
    token_block = residual_in.shape[1]
    share_size = token_block // rep_count
    own_share = lax.psum_scatter(
        projected.astype(jnp.bfloat16), ("exp", "rep"), scatter_dimension=1, tiled=True
    ).astype(jnp.float32)
    own_residual = lax.dynamic_slice_in_dim(residual_in, core_place * share_size, share_size, 1)
    own_hidden = (own_residual.astype(jnp.float32) + own_share).astype(jnp.bfloat16)
    normed = lax.all_gather(normalize(own_hidden, norm_gain), "rep", axis=1, tiled=True)
    top_count = expert_ids.shape[2]
    expert_count = lax.axis_size("ctx") * lax.axis_size("exp")
    most_rows = max(2, (token_block * top_count + expert_count - 1) // expert_count)
    capacity = requests * most_rows
    model_width = normed.shape[2]
    token_count = requests * token_block
    flat_ids = expert_ids.reshape(-1)
    row_count = flat_ids.shape[0]
    chosen = (flat_ids[:, None] == jnp.arange(expert_count, dtype=jnp.int32)[None, :]).astype(
        jnp.int32
    )
    earlier_rows = jnp.cumsum(chosen, axis=0) - chosen
    slot_rank = jnp.sum(earlier_rows * chosen, axis=1)
    slot_index = flat_ids * capacity + slot_rank
    slot_onehot = (
        slot_index[:, None] == jnp.arange(expert_count * capacity, dtype=jnp.int32)[None, :]
    ).astype(jnp.bfloat16)
    token_onehot = (
        (jnp.arange(row_count, dtype=jnp.int32) // top_count)[:, None]
        == jnp.arange(token_count, dtype=jnp.int32)[None, :]
    ).astype(jnp.bfloat16)
    placement = jnp.dot(slot_onehot.T, token_onehot, preferred_element_type=jnp.float32).astype(
        jnp.bfloat16
    )
    outgoing = jnp.dot(
        placement, normed.reshape(token_count, model_width), preferred_element_type=jnp.float32
    )
    outgoing = outgoing.astype(jnp.bfloat16).reshape(expert_count, capacity, model_width)
    scores_sum = jnp.sum(route_scores, axis=2, keepdims=True)
    combine = (route_scores / scores_sum).astype(jnp.bfloat16).reshape(-1)
    gathering = jnp.dot(
        (token_onehot * combine[:, None]).T, slot_onehot, preferred_element_type=jnp.float32
    ).astype(jnp.bfloat16)
    gate_up = expert_input[0]
    down_weight = expert_output[0]
    arrived_rows = lax.all_to_all(outgoing, ("ctx", "exp"), split_axis=0, concat_axis=0, tiled=True)
    inner_rows = jnp.einsum(
        "nd,dgh->ngh",
        arrived_rows.reshape(-1, model_width),
        gate_up,
        preferred_element_type=jnp.float32,
    )
    activated = (jax.nn.silu(inner_rows[:, 0]) * inner_rows[:, 1]).astype(jnp.bfloat16)
    result = jnp.dot(activated, down_weight, preferred_element_type=jnp.float32).astype(
        jnp.bfloat16
    )
    returned = lax.all_to_all(
        result.reshape(arrived_rows.shape), ("ctx", "exp"), split_axis=0, concat_axis=0, tiled=True
    )
    mixture = jnp.dot(
        gathering,
        returned.reshape(expert_count * capacity, model_width),
        preferred_element_type=jnp.float32,
    )
    own_mixture = lax.psum_scatter(
        mixture.reshape(requests, token_block, model_width).astype(jnp.bfloat16),
        "rep",
        scatter_dimension=1,
        tiled=True,
    ).astype(jnp.float32)
    layer_out = (own_hidden.astype(jnp.float32) + own_mixture).astype(jnp.bfloat16)
    return (context, layer_out)


def solution(mesh):
    in_specs = (
        P("groups", "ctx", ("exp", "rep")),
        P("groups", "ctx", None, "exp"),
        P("groups", None),
        P("groups", ("ctx", "exp"), None),
        P(("exp", "rep"), None),
        P(),
        P("groups", ("ctx", "exp"), None),
        P("groups", ("ctx", "exp"), None),
        P(("ctx", "exp"), None, None, "rep"),
        P(("ctx", "exp"), "rep", None),
    )
    out_specs = (P("groups", "ctx", ("exp", "rep")), P("groups", ("ctx", "exp", "rep"), None))
    return jax.shard_map(
        per_device, mesh=mesh, in_specs=in_specs, out_specs=out_specs, check_vma=False
    )
```

profile of v0, /device:TPU:0, one launch (start us, length us, event | category | flops | bytes accessed | tf_op | source)
XLA Modules:
  0.0 121.3 jit_solution(10408529155012849360)
XLA Ops:
  7.2 1.9 %copy.20 = bf16[1,576,2,128]{3,1,2,0:T(8,128)(2,1)} copy(bf16[1,576,2,128]{3,2,1,0:T(2,128)(2,1)} %param.11) | data formatting | bytes 589824 | tf_op args[1]
  9.2 0.9 copy.24
  10.1 0.8 copy.22
  11.0 0.8 select_reduce_fusion.1
  11.8 0.2 and_or_fusion
  12.0 30.6 %all-gather.2.cloned.1.call-done = bf16[1,2304,2,128]{3,1,2,0:T(8,128)(2,1)} async-done(((bf16[1,576,2,128]{3,1,2,0:T(8,128)(2,1)}), bf16[1,2304,2,128]{3,1,2,0:T(8,128)(2,1)}) %all-gather.2.cloned.1.call-update) | async-done | bytes 1179664 | tf_op jit(solution)/shard_map/all_gather | solution.py:88
  42.6 2.5 %fusion.70 = (f32[64,8]{1,0:T(8,128)S(1)}, f32[64,8,2304]{2,1,0:T(8,128)S(1)}) fusion(bf16[64,8,128]{2,1,0:T(8,128)(2,1)S(1)} %bitcast.57, bf16[1,2304,2,128]{3,1,2,0:T(8,128)(2,1)} %all-gather.2.cloned.1.call-done, pred[64,2304]{1,0:T(8,128)(4,1)S(1)} %and_or_fusion), kind=kOutput, calls=%fused_computation.88 | convolution fusion | flops 305528320 | bytes 5588992 | tf_op jit(solution)/shard_map/rqhe,rke->rqhk/dot_general | solution.py:20
  45.1 1.3 %fusion.1 = f32[64,8]{1,0:T(8,128)S(1)} fusion(f32[64,8,2304]{2,1,0:T(8,128)S(1)} %get-tuple-element.5, f32[64,8]{1,0:T(8,128)S(1)} %get-tuple-element.4, pred[64,2304]{1,0:T(8,128)(4,1)S(1)} %and_or_fusion), kind=kLoop, calls=%fused_computation.3 | loop fusion | flops 3538432 | bytes 4870144 | tf_op jit(solution)/shard_map/reduce_sum | solution.py:29
  46.4 1.1 fusion.24
  47.5 1.0 copy-done.1
  48.5 1.5 %fusion.12 = bf16[1,64,2048]{2,1,0:T(8,128)(2,1)} fusion(bf16[1024,2048]{1,0:T(8,128)(2,1)S(1)} %copy-done.1, bf16[8,8,8,128]{3,2,1,0:T(8,128)(2,1)S(1)} %bitcast.56), kind=kOutput, calls=%fused_computation.16 | convolution fusion | flops 268566528 | bytes 4587520 | tf_op jit(solution)/shard_map/dot_general | solution.py:99
  50.2 0.2 reduce_window_sum.11
  50.4 0.2 select_reduce_fusion
  50.6 19.0 %reduce-scatter.2.cloned.1.call-done = bf16[1,16,2048]{2,1,0:T(8,128)(2,1)} async-done(((bf16[1,64,2048]{2,1,0:T(8,128)(2,1)}), bf16[1,16,2048]{2,1,0:T(8,128)(2,1)}) %reduce-scatter.2.cloned.1.call-update) | async-done | bytes 65552 | tf_op jit(solution)/shard_map/reduce_scatter | solution.py:106
  69.6 1.0 fusion.30
  70.6 2.2 %fusion.10 = bf16[16,8,2048]{2,1,0:T(8,128)(2,1)} fusion(f32[2048]{0:T(1024)S(1)} %copy-done.7, f32[16]{0:T(128)S(1)} %add_rsqrt_fusion, s32[128]{0:T(128)S(1)} %get-tuple-element.9, s32[128]{0:T(128)S(1)} %get-tuple-element.8, bf16[1,16,2048]{2,1,0:T(8,128)(2,1)} %reduce-scatter.2.cloned.1.call-done, bf16[1,16,2048]{2,1,0:T(8,128)(2,1)S(1)} %copy-done.3), kind=kOutput, calls=%fused_computation.13 | convolution fusion | flops 9457664 | bytes 664640 | tf_op jit(solution)/shard_map/dot_general | solution.py:136
  72.8 19.1 %all_to_all.10 = bf16[16,8,2048]{2,1,0:T(8,128)(2,1)S(1)} all-to-all(bf16[16,8,2048]{2,1,0:T(8,128)(2,1)} %fusion.10), channel_id=1, replica_groups=mesh['groups'=2,'ctx'=4,'exp'=4,'rep'=1] {'ctx','exp'}, dimensions={0} | all-to-all | bytes 1048576 | tf_op jit(solution)/shard_map/all_to_all | solution.py:147
  91.9 0.6 fusion.3
  92.5 1.3 %fusion.11 = bf16[16,8,2048]{2,1,0:T(8,128)(2,1)} fusion(bf16[1,384,2048]{2,1,0:T(8,128)(2,1)S(1)} %copy-done.2, f32[128,2,384]{2,0,1:T(8,128)S(1)} %fusion.3), kind=kOutput, calls=%fused_computation.14 | convolution fusion | flops 201883648 | bytes 2490368 | tf_op jit(solution)/shard_map/dot_general | solution.py:155
  93.8 4.2 %all-to-all-start.1 = ((bf16[16,8,2048]{2,1,0:T(8,128)(2,1)}), bf16[16,8,2048]{2,1,0:T(8,128)(2,1)}, u32[]{:S(2)}, u32[]{:S(2)}) async-start(bf16[16,8,2048]{2,1,0:T(8,128)(2,1)} %fusion.11), calls=%async_computation.2 | async-start | bytes 1048576 | tf_op jit(solution)/shard_map/all_to_all | solution.py:158
  98.2 0.1 mul.119
  98.3 0.7 reshape.326
  99.0 13.4 %all-to-all-done.1 = bf16[16,8,2048]{2,1,0:T(8,128)(2,1)} async-done(((bf16[16,8,2048]{2,1,0:T(8,128)(2,1)}), bf16[16,8,2048]{2,1,0:T(8,128)(2,1)}, u32[]{:S(2)}, u32[]{:S(2)}) %all-to-all-start.1) | async-done | bytes 524320 | tf_op jit(solution)/shard_map/all_to_all | solution.py:158
  112.4 2.1 %fusion.16 = bf16[1,16,2048]{2,1,0:T(8,128)(2,1)} fusion(bf16[16,8,2048]{2,1,0:T(8,128)(2,1)} %all-to-all-done.1, s32[128]{0:T(128)S(1)} %get-tuple-element.9, s32[128]{0:T(128)S(1)} %get-tuple-element.8, bf16[128]{0:T(256)(128)(2,1)S(1)} %mul.119, bf16[1,16,2048]{2,1,0:T(8,128)(2,1)S(1)} %copy-done.4, bf16[1,16,2048]{2,1,0:T(8,128)(2,1)S(1)} %copy-done.3), kind=kOutput, calls=%fused_computation.21 | convolution fusion | flops 9230336 | bytes 722176 | tf_op jit(solution)/shard_map/dot_general | solution.py:161
  (31 shorter events, 0.5 us)
Async XLA Ops:
  7.2 84.7 %copy-start = (bf16[1,2048,2,384]{3,2,1,0:T(2,128)(2,1)S(1)}, bf16[1,2048,2,384]{3,2,1,0:T(2,128)(2,1)}, u32[]{:S(2)}) copy-start(bf16[1,2048,2,384]{3,2,1,0:T(2,128)(2,1)} %param.18) | copy-start | bytes 9437188
  7.2 35.4 %all-gather.2.cloned.1.call-start = ((), (), s32[]{:S(2)}) async-start(), calls=%async_computation.3 | async-start | bytes 1474560 | tf_op jit(solution)/shard_map/all_gather | solution.py:88
  9.1 60.5 %reduce-scatter.2.cloned.1.call-start = ((), (), s32[]{:S(2)}) async-start(), calls=%async_computation.4 | async-start | bytes 327680 | tf_op jit(solution)/shard_map/reduce_scatter | solution.py:106
  42.6 3.8 %copy-start.5 = (bf16[1,2304,2,128]{3,1,2,0:T(8,128)(2,1)S(1)}, bf16[1,2304,2,128]{3,1,2,0:T(8,128)(2,1)}, u32[]{:S(2)}) copy-start(bf16[1,2304,2,128]{3,1,2,0:T(8,128)(2,1)} %all-gather.2.cloned.1.call-done) | copy-start | bytes 3538948
  46.4 2.2 %copy-start.1 = (bf16[1024,2048]{1,0:T(8,128)(2,1)S(1)}, bf16[1024,2048]{1,0:T(8,128)(2,1)}, u32[]{:S(2)}) copy-start(bf16[1024,2048]{1,0:T(8,128)(2,1)} %param.14) | copy-start | bytes 12582916
  47.5 22.1 %copy-start.3 = (bf16[1,16,2048]{2,1,0:T(8,128)(2,1)S(1)}, bf16[1,16,2048]{2,1,0:T(8,128)(2,1)}, u32[]{:S(2)}) copy-start(bf16[1,16,2048]{2,1,0:T(8,128)(2,1)} %param.13) | copy-start | bytes 196612
  47.5 23.1 %copy-start.7 = (f32[2048]{0:T(1024)S(1)}, f32[2048]{0:T(1024)}, u32[]{:S(2)}) copy-start(f32[2048]{0:T(1024)} %param.15) | copy-start | bytes 24580
  72.8 19.8 %copy-start.2 = (bf16[1,384,2048]{2,1,0:T(8,128)(2,1)S(1)}, bf16[1,384,2048]{2,1,0:T(8,128)(2,1)}, u32[]{:S(2)}) copy-start(bf16[1,384,2048]{2,1,0:T(8,128)(2,1)} %param.19) | copy-start | bytes 4718596
  91.9 6.2 %copy-start.6 = (f32[1,16,8]{1,2,0:T(8,128)S(1)}, f32[1,16,8]{1,2,0:T(8,128)}, u32[]{:S(2)}) copy-start(f32[1,16,8]{1,2,0:T(8,128)} %param.17) | copy-start | bytes 1540
  91.9 20.5 %copy-start.4 = (bf16[1,16,2048]{2,1,0:T(8,128)(2,1)S(1)}, bf16[1,16,2048]{2,1,0:T(8,128)(2,1)}, u32[]{:S(2)}) copy-start(bf16[1,16,2048]{2,1,0:T(8,128)(2,1)} %reduce-scatter.2.cloned.1.call-done) | copy-start | bytes 196612
  93.8 18.6 %all-to-all-start.1 = ((bf16[16,8,2048]{2,1,0:T(8,128)(2,1)}), bf16[16,8,2048]{2,1,0:T(8,128)(2,1)}, u32[]{:S(2)}, u32[]{:S(2)}) async-start(bf16[16,8,2048]{2,1,0:T(8,128)(2,1)} %fusion.11), calls=%async_computation.2 | async-start | bytes 1048576 | tf_op jit(solution)/shard_map/all_to_all | solution.py:158
Sparse Core Ops, SparseCore 0:
  9.6 32.9 all-gather.1
  50.2 19.2 reduce-scatter.1
where the time goes:
time: 122 us; the launch traced here: 121 us
  waiting for transfers between devices  63 us (52%)
  blocking collectives  19.1 us (16%)
  between operations  14.2 us (12%)
  matrix products  11.3 us (9%)
  local copies, waits for them, and re-layouts  5.62 us (5%)
  starting transfers between devices  4.32 us (4%)
  other arithmetic  3.74 us (3%)
    all_gather x1, waiting for transfers between devices, per_device(): page_piece = lax.all_gather(pages, 'ctx', axis=1, tiled=True)  30.6 us
    all_to_all x1, blocking collectives, per_device(): lax.all_to_all(outgoing, ('ctx', 'exp'), split_axis=0, concat_axis=0, til...  19.1 us
    reduce_scatter x1, waiting for transfers between devices, per_device(): lax.psum_scatter(projected.astype(jnp.bfloat16), ('exp', 'rep'), scatter_...  19 us
    all_to_all x1, waiting for transfers between devices, per_device(): lax.all_to_all(result.reshape(arrived_rows.shape), ('ctx', 'exp'), split_...  13.4 us
    unnamed x19, local copies, waits for them, and re-layouts  4.63 us
    all_to_all x1, starting transfers between devices, per_device(): lax.all_to_all(result.reshape(arrived_rows.shape), ('ctx', 'exp'), split_...  4.24 us
    dot_general x1, matrix products, attend_piece(): jnp.einsum('rqhe,rke->rqhk', query_rows, page_rows[:, :, 0], preferred_el...  2.46 us
  transfers between devices with their start and end apart: 3, of which 3 were waited for; matrix products, arithmetic and copies ran while one was open for 3% of the time, Pallas kernels for 0%

commit v1 on v0

--- a/solution.py
+++ b/solution.py
@@ -6,6 +6,18 @@
 HEAD = 128
 floor_value = -1e30
 norm_epsilon = 1e-06
+
+
+def gather_by_bits(x, axis, dim):
+    ways, here = (lax.axis_size(axis), lax.axis_index(axis))
+    grown, reach = (x, 1)
+    while reach < ways:
+        theirs = lax.ppermute(grown, axis, [(d, d ^ reach) for d in range(ways)])
+        mine_first = jnp.concatenate([grown, theirs], axis=dim)
+        theirs_first = jnp.concatenate([theirs, grown], axis=dim)
+        grown = jnp.where(here & reach == 0, mine_first, theirs_first)
+        reach = 2 * reach
+    return grown
 
 
 def normalize(hidden, norm_gain):
@@ -85,7 +97,7 @@
         jnp.zeros((requests, fresh_block, local_heads), jnp.float32),
         jnp.zeros((requests, fresh_block, local_heads, HEAD), jnp.float32),
     )
-    page_piece = lax.all_gather(pages, "ctx", axis=1, tiled=True)
+    page_piece = gather_by_bits(pages, "ctx", 1)
     row_index = jnp.arange(page_piece.shape[1], dtype=jnp.int32)
     allowed = rows_mask(row_index, cached_lengths, own_positions, slab_size, fresh_block)
     peaks, totals, summed = merge_partials(

time: 122 us -> 128 us (1.049)
  starting transfers between devices: 4.32 us -> 10.2 us
  other arithmetic: 3.74 us -> 6.27 us
  matrix products: 11.3 us -> 9.73 us
    all_gather x1 -> x0, waiting for transfers between devices: 30.6 us -> none  [per_device(): page_piece = lax.all_gather(pages, 'ctx', axis=1, tiled=True)]
    ppermute x0 -> x2, waiting for transfers between devices: none -> 27.7 us  [gather_by_bits(): theirs = lax.ppermute(grown, axis, [(d, d ^ reach) for d in range(ways)])]
    ppermute x0 -> x2, starting transfers between devices: none -> 5.93 us  [gather_by_bits(): theirs = lax.ppermute(grown, axis, [(d, d ^ reach) for d in range(ways)])]
    reduce_scatter x1, waiting for transfers between devices: 19 us -> 20.8 us  [per_device(): lax.psum_scatter(projected.astype(jnp.bfloat16), ('exp', 'rep'), scatter_...]
    select_n x0 -> x2, other arithmetic: none -> 1.51 us  [gather_by_bits(): grown = jnp.where(here & reach == 0, mine_first, theirs_first)]
    dot_general x1, matrix products: 2.46 us -> 1.08 us  [attend_piece(): jnp.einsum('rqhe,rke->rqhk', query_rows, page_rows[:, :, 0], preferred_el...]
  transfers between devices with their start and end apart: 3 -> 4, of which waited for: 3 -> 4; matrix products, arithmetic and copies ran while one was open for 3% -> 5% of each run, Pallas kernels for 0% -> 0%
where the time goes in v1:
time: 128 us
  waiting for transfers between devices  61.8 us (48%)
  blocking collectives  19 us (15%)
  between operations  14.2 us (11%)
  starting transfers between devices  10.2 us (8%)
  matrix products  9.73 us (8%)
  local copies, waits for them, and re-layouts  6.68 us (5%)
  other arithmetic  6.27 us (5%)
    ppermute x2, waiting for transfers between devices, gather_by_bits(): theirs = lax.ppermute(grown, axis, [(d, d ^ reach) for d in range(ways)])  27.7 us
    reduce_scatter x1, waiting for transfers between devices, per_device(): lax.psum_scatter(projected.astype(jnp.bfloat16), ('exp', 'rep'), scatter_...  20.8 us
    all_to_all x1, blocking collectives, per_device(): lax.all_to_all(outgoing, ('ctx', 'exp'), split_axis=0, concat_axis=0, til...  19 us
    all_to_all x1, waiting for transfers between devices, per_device(): lax.all_to_all(result.reshape(arrived_rows.shape), ('ctx', 'exp'), split_...  13.3 us
    ppermute x2, starting transfers between devices, gather_by_bits(): theirs = lax.ppermute(grown, axis, [(d, d ^ reach) for d in range(ways)])  5.93 us
    unnamed x19, local copies, waits for them, and re-layouts  5.6 us
    all_to_all x1, starting transfers between devices, per_device(): lax.all_to_all(result.reshape(arrived_rows.shape), ('ctx', 'exp'), split_...  4.24 us
  transfers between devices with their start and end apart: 4, of which 4 were waited for; matrix products, arithmetic and copies ran while one was open for 5% of the time, Pallas kernels for 0%

profile of v1, /device:TPU:0, one launch (start us, length us, event | category | flops | bytes accessed | tf_op | source)
XLA Modules:
  0.0 127.9 jit_solution(17683285578803037300)
XLA Ops:
  7.2 1.2 copy.66
  8.4 3.1 %collective-permute-start = (bf16[1,576,2,128]{3,1,2,0:T(8,128)(2,1)S(1)}, bf16[1,576,2,128]{3,1,2,0:T(8,128)(2,1)}, u32[]{:S(2)}, u32[]{:S(2)}) collective-permute-start(bf16[1,576,2,128]{3,1,2,0:T(8,128)(2,1)S(1)} %copy.66), channel_id=1, source_target_pairs={{0,4},{4,0},{8,12},{12,8},{1,5},{5,1},{9,13},{13,9},{2,6},{6,2},{1... | collective-permute-start | bytes 884744 | tf_op jit(solution)/shard_map/ppermute | solution.py:15
  11.5 1.6 %copy.53 = bf16[8,8,8,128]{3,2,1,0:T(8,128)(2,1)} copy(bf16[8,8,8,128]{3,1,2,0:T(8,128)(2,1)} %bitcast.69) | data formatting | bytes 262144
  13.1 0.8 copy.50
  14.0 0.8 select_reduce_fusion.1
  14.8 3.8 %collective-permute-done = bf16[1,576,2,128]{3,1,2,0:T(8,128)(2,1)} collective-permute-done((bf16[1,576,2,128]{3,1,2,0:T(8,128)(2,1)S(1)}, bf16[1,576,2,128]{3,1,2,0:T(8,128)(2,1)}, u32[]{:S(2)}, u32[]{:S(2)}) %collective-permute-start) | collective-permute-done | bytes 294944 | tf_op jit(solution)/shard_map/ppermute | solution.py:15
  18.6 1.2 maximum_select_fusion.2
  19.8 2.8 %collective-permute-start.1 = (bf16[1,1152,2,128]{3,1,2,0:T(8,128)(2,1)S(1)}, bf16[1,1152,2,128]{3,1,2,0:T(8,128)(2,1)S(1)}, u32[]{:S(2)}, u32[]{:S(2)}) collective-permute-start(bf16[1,1152,2,128]{3,1,2,0:T(8,128)(2,1)S(1)} %maximum_select_fusion.2), channel_id=1, source_target_pairs={{0,8},{4,12},{8,0},{12,4},{1,9},{5,13},{9,1},{13,5},{2,10},{6,14},... | collective-permute-start | bytes 1769480 | tf_op jit(solution)/shard_map/ppermute | solution.py:15
  22.8 1.2 fusion.28
  24.0 23.9 %collective-permute-done.1 = bf16[1,1152,2,128]{3,1,2,0:T(8,128)(2,1)S(1)} collective-permute-done((bf16[1,1152,2,128]{3,1,2,0:T(8,128)(2,1)S(1)}, bf16[1,1152,2,128]{3,1,2,0:T(8,128)(2,1)S(1)}, u32[]{:S(2)}, u32[]{:S(2)}) %collective-permute-start.1) | collective-permute-done | bytes 589856 | tf_op jit(solution)/shard_map/ppermute | solution.py:15
  48.2 1.1 fusion.73
  49.3 1.1 fusion.2
  50.4 0.9 fusion.25
  51.3 1.3 %copy-done.1 = bf16[1024,2048]{1,0:T(8,128)(2,1)S(1)} copy-done((bf16[1024,2048]{1,0:T(8,128)(2,1)S(1)}, bf16[1024,2048]{1,0:T(8,128)(2,1)}, u32[]{:S(2)}) %copy-start.1) | copy-done | bytes 4194328
  52.6 1.6 %fusion.13 = bf16[1,64,2048]{2,1,0:T(8,128)(2,1)} fusion(bf16[1024,2048]{1,0:T(8,128)(2,1)S(1)} %copy-done.1, bf16[64,8,128]{2,0,1:T(8,128)(2,1)S(1)} %fusion.25), kind=kOutput, calls=%fused_computation.17 | convolution fusion | flops 268566528 | bytes 4587520 | tf_op jit(solution)/shard_map/dot_general | solution.py:111
  54.7 20.8 %reduce-scatter.2.cloned.1.call-done = bf16[1,16,2048]{2,1,0:T(8,128)(2,1)} async-done(((bf16[1,64,2048]{2,1,0:T(8,128)(2,1)}), bf16[1,16,2048]{2,1,0:T(8,128)(2,1)}) %reduce-scatter.2.cloned.1.call-update) | async-done | bytes 65552 | tf_op jit(solution)/shard_map/reduce_scatter | solution.py:118
  75.5 1.0 fusion.32
  76.5 2.2 %fusion.11 = bf16[16,8,2048]{2,1,0:T(8,128)(2,1)} fusion(f32[2048]{0:T(1024)S(1)} %copy-done.7, f32[16]{0:T(128)S(1)} %add_rsqrt_fusion, s32[128]{0:T(128)S(1)} %get-tuple-element.11, s32[128]{0:T(128)S(1)} %get-tuple-element.10, bf16[1,16,2048]{2,1,0:T(8,128)(2,1)} %reduce-scatter.2.cloned.1.call-done, bf16[1,16,2048]{2,1,0:T(8,128)(2,1)S(1)} %copy-done.3), kind=kOutput, calls=%fused_computation.14 | convolution fusion | flops 9457664 | bytes 664640 | tf_op jit(solution)/shard_map/dot_general | solution.py:148
  78.7 19.0 %all_to_all.10 = bf16[16,8,2048]{2,1,0:T(8,128)(2,1)S(1)} all-to-all(bf16[16,8,2048]{2,1,0:T(8,128)(2,1)} %fusion.11), channel_id=1, replica_groups=mesh['groups'=2,'ctx'=4,'exp'=4,'rep'=1] {'ctx','exp'}, dimensions={0} | all-to-all | bytes 1048576 | tf_op jit(solution)/shard_map/all_to_all | solution.py:159
  98.3 0.8 copy-done.2
  99.1 1.3 fusion.12
  100.4 4.2 %all-to-all-start.1 = ((bf16[16,8,2048]{2,1,0:T(8,128)(2,1)}), bf16[16,8,2048]{2,1,0:T(8,128)(2,1)}, u32[]{:S(2)}, u32[]{:S(2)}) async-start(bf16[16,8,2048]{2,1,0:T(8,128)(2,1)} %fusion.12), calls=%async_computation.2 | async-start | bytes 1048576 | tf_op jit(solution)/shard_map/all_to_all | solution.py:170
  105.6 13.3 %all-to-all-done.1 = bf16[16,8,2048]{2,1,0:T(8,128)(2,1)} async-done(((bf16[16,8,2048]{2,1,0:T(8,128)(2,1)}), bf16[16,8,2048]{2,1,0:T(8,128)(2,1)}, u32[]{:S(2)}, u32[]{:S(2)}) %all-to-all-start.1) | async-done | bytes 524320 | tf_op jit(solution)/shard_map/all_to_all | solution.py:170
  118.9 2.1 %fusion.17 = bf16[1,16,2048]{2,1,0:T(8,128)(2,1)} fusion(bf16[16,8,2048]{2,1,0:T(8,128)(2,1)} %all-to-all-done.1, s32[128]{0:T(128)S(1)} %get-tuple-element.11, s32[128]{0:T(128)S(1)} %get-tuple-element.10, bf16[128]{0:T(256)(128)(2,1)S(1)} %mul.123, bf16[1,16,2048]{2,1,0:T(8,128)(2,1)S(1)} %copy-done.4, bf16[1,16,2048]{2,1,0:T(8,128)(2,1)S(1)} %copy-done.3), kind=kOutput, calls=%fused_computation.22 | convolution fusion | flops 9230336 | bytes 722176 | tf_op jit(solution)/shard_map/dot_general | solution.py:173
  (36 shorter events, 2.8 us)
Async XLA Ops:
  7.2 90.5 %copy-start = (bf16[1,2048,2,384]{3,2,1,0:T(2,128)(2,1)S(1)}, bf16[1,2048,2,384]{3,2,1,0:T(2,128)(2,1)}, u32[]{:S(2)}) copy-start(bf16[1,2048,2,384]{3,2,1,0:T(2,128)(2,1)} %param.18) | copy-start | bytes 9437188
  7.2 68.3 %reduce-scatter.2.cloned.1.call-start = ((), (), s32[]{:S(2)}) async-start(), calls=%async_computation.3 | async-start | bytes 327680 | tf_op jit(solution)/shard_map/reduce_scatter | solution.py:118
  8.4 10.2 %collective-permute-start = (bf16[1,576,2,128]{3,1,2,0:T(8,128)(2,1)S(1)}, bf16[1,576,2,128]{3,1,2,0:T(8,128)(2,1)}, u32[]{:S(2)}, u32[]{:S(2)}) collective-permute-start(bf16[1,576,2,128]{3,1,2,0:T(8,128)(2,1)S(1)} %copy.66), channel_id=1, source_target_pairs={{0,4},{4,0},{8,12},{12,8},{1,5},{5,1},{9,13},{13,9},{2,6},{6,2},{1... | collective-permute-start | bytes 884744 | tf_op jit(solution)/shard_map/ppermute | solution.py:15
  14.8 33.5 %copy-start.5 = (bf16[8,8,8,128]{3,2,1,0:T(8,128)(2,1)S(1)}, bf16[8,8,8,128]{3,2,1,0:T(8,128)(2,1)}, u32[]{:S(2)}) copy-start(bf16[8,8,8,128]{3,2,1,0:T(8,128)(2,1)} %copy.53) | copy-start | bytes 393220
  19.8 28.1 %collective-permute-start.1 = (bf16[1,1152,2,128]{3,1,2,0:T(8,128)(2,1)S(1)}, bf16[1,1152,2,128]{3,1,2,0:T(8,128)(2,1)S(1)}, u32[]{:S(2)}, u32[]{:S(2)}) collective-permute-start(bf16[1,1152,2,128]{3,1,2,0:T(8,128)(2,1)S(1)} %maximum_select_fusion.2), channel_id=1, source_target_pairs={{0,8},{4,12},{8,0},{12,4},{1,9},{5,13},{9,1},{13,5},{2,10},{6,14},... | collective-permute-start | bytes 1769480 | tf_op jit(solution)/shard_map/ppermute | solution.py:15
  50.4 2.2 %copy-start.1 = (bf16[1024,2048]{1,0:T(8,128)(2,1)S(1)}, bf16[1024,2048]{1,0:T(8,128)(2,1)}, u32[]{:S(2)}) copy-start(bf16[1024,2048]{1,0:T(8,128)(2,1)} %param.14) | copy-start | bytes 12582916
  52.6 22.8 %copy-start.3 = (bf16[1,16,2048]{2,1,0:T(8,128)(2,1)S(1)}, bf16[1,16,2048]{2,1,0:T(8,128)(2,1)}, u32[]{:S(2)}) copy-start(bf16[1,16,2048]{2,1,0:T(8,128)(2,1)} %param.13) | copy-start | bytes 196612
  52.6 23.8 %copy-start.7 = (f32[2048]{0:T(1024)S(1)}, f32[2048]{0:T(1024)}, u32[]{:S(2)}) copy-start(f32[2048]{0:T(1024)} %param.15) | copy-start | bytes 24580
  97.7 1.4 %copy-start.2 = (bf16[1,384,2048]{2,1,0:T(8,128)(2,1)S(1)}, bf16[1,384,2048]{2,1,0:T(8,128)(2,1)}, u32[]{:S(2)}) copy-start(bf16[1,384,2048]{2,1,0:T(8,128)(2,1)} %param.19) | copy-start | bytes 4718596
  99.1 5.5 %copy-start.6 = (f32[1,16,8]{1,2,0:T(8,128)S(1)}, f32[1,16,8]{1,2,0:T(8,128)}, u32[]{:S(2)}) copy-start(f32[1,16,8]{1,2,0:T(8,128)} %param.17) | copy-start | bytes 1540
  99.1 19.8 %copy-start.4 = (bf16[1,16,2048]{2,1,0:T(8,128)(2,1)S(1)}, bf16[1,16,2048]{2,1,0:T(8,128)(2,1)}, u32[]{:S(2)}) copy-start(bf16[1,16,2048]{2,1,0:T(8,128)(2,1)} %reduce-scatter.2.cloned.1.call-done) | copy-start | bytes 196612
  100.4 18.5 %all-to-all-start.1 = ((bf16[16,8,2048]{2,1,0:T(8,128)(2,1)}), bf16[16,8,2048]{2,1,0:T(8,128)(2,1)}, u32[]{:S(2)}, u32[]{:S(2)}) async-start(bf16[16,8,2048]{2,1,0:T(8,128)(2,1)} %fusion.12), calls=%async_computation.2 | async-start | bytes 1048576 | tf_op jit(solution)/shard_map/all_to_all | solution.py:170
Sparse Core Ops, SparseCore 0:
  54.3 21.0 reduce-scatter.1
